TPU v7x, 512 devices: a whole 4x8x8 slice. The times are simulated.
512 devices in a mesh: dp: 16 (over z, core), tp: 32 (over y, x).
Axes of the slice: x: 4, y: 8, z: 8, core: 2. Of those that a mesh axis runs over, the one named last changes fastest.
Arguments:
- q_new: bfloat16 [512, 1536], P(('dp', 'tp'))
- new_key_value: bfloat16 [512, 512], P(('dp', 'tp')), may hold values from -6 to 6
- resid_dec: bfloat16 [512, 1536], P(('dp', 'tp')), may hold values from -6 to 6
- placing: int32 [512], replicated, may hold values from 0 to 511, as said below
- lengths: int32 [512], P('dp'), may hold values from 5 to 2048, as said below
- write_pos: int32 [512], P('dp'), may hold values from 4 to 2047, as said below
- k_cache: bfloat16 [512, 2, 2048, 128], P('dp', None, 'tp')
- value_cache: bfloat16 [512, 2, 2048, 128], P('dp', None, 'tp'), may hold values from -6 to 6
- w_out: bfloat16 [1536, 1536], P(None, 'tp'), may hold values from -0.15625 to 0.15625
- x_pre: bfloat16 [32256, 1536], P(('dp', 'tp')), may hold values from -6 to 6
- routes: int32 [32768, 4], P(('dp', 'tp')), may hold values from 0 to 31, all different within a row; in each aligned block of 64 rows (0 to 63, 64 to 127, ...) at most 16 rows name the same one
- route_scale: float32 [32768, 4], P(('dp', 'tp')), may hold values from 0.2 to 2
- moe_gain: float32 [1536], replicated, may hold values from 0.5 to 1.5
- w_gate: bfloat16 [32, 768, 1536], P('tp', 'dp'), may hold values from -0.15625 to 0.15625
- w_up: bfloat16 [32, 768, 1536], P('tp', 'dp'), may hold values from -0.15625 to 0.15625
- w_down: bfloat16 [32, 768, 1536], P('tp', 'dp'), may hold values from -0.21875 to 0.21875
Outputs:
- out_pre: bfloat16 [32256, 1536], P(('dp', 'tp'))
- out_dec: bfloat16 [512, 1536], P(('dp', 'tp'))
Inputs may be any that keep to these rules, and one draw needn't show every extreme that they name: Each of 0 to 511 appears once; cache row j belongs to request placing[j]. `lengths`: a cache row is either full (2048 live slots) or filled from slot 0 up; some row is full. `write_pos`: below the row's length; a row that is not full writes at its length - 1, a full row anywhere past the sink slots. `routes`: the 64 rows of one device name any one expert at most 16 times.
All inputs are finite; a program needn't handle non-finite values.
Results may differ from a plain program's by a relative error of at most 0.007.
Values may be sent and summed in bfloat16 or wider, within the bound.
No kernel may reach another device: no remote copies, remote signals or barrier semaphores. Data moves between devices by JAX's collectives and lax.ppermute only.
A program may use at most 64 MiB of HBM per device.

v0:
```python
import jax
import jax.numpy as jnp
from jax import lax
from jax.sharding import PartitionSpec as P

HIGHEST = lax.Precision.HIGHEST
F32 = jnp.float32
BF16 = jnp.bfloat16


def contract_rows(left_rows, unit_rows):
    return lax.dot_general(
        left_rows, unit_rows, (((1,), (1,)), ((), ())), preferred_element_type=F32
    )


def swap(blocks, axis_name):
    return lax.all_to_all(blocks, axis_name, split_axis=0, concat_axis=0, tiled=True)


def spread(block, axis_name):
    members = lax.axis_size(axis_name)
    return swap(jnp.broadcast_to(block[None], (members,) + block.shape), axis_name)


def choose_rows(table, rows):
    return jnp.dot(table.astype(BF16), rows, preferred_element_type=F32).astype(BF16)


def pieces_of(x):
    high = lax.reduce_precision(x, 8, 7)
    middle = lax.reduce_precision(x - high, 8, 7)
    low = lax.reduce_precision(x - high - middle, 8, 7)
    return (high.astype(BF16), middle.astype(BF16), low.astype(BF16))


def rms(rows_f32, gain):
    mean_square = jnp.mean(rows_f32 * rows_f32, axis=-1, keepdims=True)
    return (rows_f32 * lax.rsqrt(mean_square + 1e-06) * gain).astype(BF16)


def expert_units(rows, units):
    gate = contract_rows(rows, units[0])
    upper = contract_rows(rows, units[1])
    active = (jnp.maximum(gate, 0.0) * upper).astype(BF16)
    return jnp.dot(active, units[2], preferred_element_type=F32).astype(BF16)


def on_device(
    q_new,
    new_key_value,
    resid_dec,
    placing,
    lengths,
    write_pos,
    k_cache,
    value_cache,
    w_out,
    x_pre,
    routes,
    route_scale,
    moe_gain,
    w_gate,
    w_up,
    w_down,
):
    dp_size = lax.axis_size("dp")
    tp_size = lax.axis_size("tp")
    dp_group = lax.axis_index("dp")
    tp_lane = lax.axis_index("tp")
    group_reqs, kv_heads, slot_dev, head_size = k_cache.shape
    width = q_new.shape[1]
    heads = width // head_size
    per_group = heads // kv_heads
    total_reqs = placing.shape[0]
    experts = tp_size * w_gate.shape[0]
    assert group_reqs == tp_size and experts == tp_size
    out_rows = lax.all_gather(w_out.T, "tp", axis=0, tiled=True)
    stacked = jnp.concatenate([w_gate, w_up, w_down], axis=0)
    stacked, _ = lax.optimization_barrier((stacked, out_rows))
    units = lax.all_gather(stacked, "dp", axis=1, tiled=True)
    columns = heads + 2 * kv_heads
    share = tp_size // columns
    chosen_rows = group_reqs // share
    fresh = jnp.concatenate([q_new, new_key_value], axis=1).reshape(1, columns, 1, head_size)
    by_head = swap(
        jnp.broadcast_to(fresh, (share, columns, 1, head_size)).reshape(tp_size, 1, head_size), "tp"
    )
    all_rows = spread(by_head.reshape(tp_size, head_size), "dp").reshape(total_reqs, head_size)
    first_row = dp_group * group_reqs + tp_lane // columns * chosen_rows
    wanted = lax.dynamic_slice_in_dim(placing, first_row, chosen_rows)
    request_ids = jnp.arange(total_reqs, dtype=jnp.int32)
    mine = choose_rows(wanted[:, None] == request_ids[None, :], all_rows)
    heads_here = spread(mine, "tp").reshape(share, columns, chosen_rows, head_size)
    cached = jnp.transpose(heads_here, (0, 2, 1, 3)).reshape(group_reqs, columns, head_size)
    query_head_list = cached[:, :heads].reshape(group_reqs, kv_heads, per_group, head_size)
    incoming_key = cached[:, heads : heads + kv_heads][:, :, None, :]
    incoming_value = cached[:, heads + kv_heads :][:, :, None, :]
    slot_ids = tp_lane * slot_dev + jnp.arange(slot_dev, dtype=jnp.int32)
    written = (slot_ids[None, :] == write_pos[:, None])[:, None, :, None]
    key_rows = jnp.where(written, incoming_key, k_cache)
    value_rows = jnp.where(written, incoming_value, value_cache).astype(F32)
    scores = jnp.einsum(
        "rgqd,rgsd->rgqs", query_head_list, key_rows, preferred_element_type=F32
    ) * head_size ** (-0.5)
    is_valid = (slot_ids[None, :] < lengths[:, None])[:, None, None, :]
    masked = jnp.where(is_valid, scores, -1e30)
    local_peak = jnp.max(masked, axis=-1)
    weights = jnp.where(is_valid, jnp.exp(masked - local_peak[..., None]), 0.0)
    local_total = jnp.sum(weights, axis=-1)
    local_mixed = jnp.einsum("rgqs,rgsd->rgqd", weights, value_rows, precision=HIGHEST)

    def lane_row(values):
        row = jnp.concatenate(pieces_of(values.reshape(group_reqs, heads)), axis=1)
        return jnp.pad(row, ((0, 0), (0, head_size - row.shape[1])))[:, None, :]

    parts = jnp.concatenate(
        [
            local_mixed.reshape(group_reqs, heads, head_size).astype(BF16),
            lane_row(local_peak),
            lane_row(local_total),
            jnp.zeros((group_reqs, 2, head_size), BF16),
        ],
        axis=1,
    )
    gathered = swap(parts, "tp")
    tail = gathered[:, heads : heads + 2, : 3 * heads].astype(F32)
    tail = tail[..., :heads] + tail[..., heads : 2 * heads] + tail[..., 2 * heads :]
    peaks, totals = (tail[:, 0], tail[:, 1])
    scale = jnp.exp(peaks - jnp.max(peaks, axis=0, keepdims=True))
    total = jnp.sum(scale * totals, axis=0)
    mixed = jnp.sum(scale[:, :, None] * gathered[:, :heads].astype(F32), axis=0)
    attention_row = (mixed / total[:, None]).astype(BF16)
    projected = contract_rows(attention_row.reshape(1, width), out_rows).astype(BF16)
    request = lax.dynamic_slice_in_dim(placing, dp_group * group_reqs + tp_lane, 1)[0]
    lane_of = jnp.arange(tp_size, dtype=jnp.int32) == request % tp_size
    no_value = jnp.zeros((), BF16)
    by_lane = swap(
        jnp.where(lane_of[:, None], projected, no_value).reshape(tp_size, heads, head_size), "tp"
    )
    group_rows = lax.dynamic_slice_in_dim(placing, dp_group * group_reqs, group_reqs)
    here = group_rows % tp_size == tp_lane
    to_group = (group_rows // tp_size)[None, :] == jnp.arange(dp_size, dtype=jnp.int32)[:, None]
    outbound = choose_rows(to_group & here[None, :], by_lane.reshape(tp_size, width))
    inbound = swap(outbound.reshape(dp_size, heads, head_size), "dp").reshape(dp_size, width)
    home_ids = dp_group * tp_size + tp_lane
    source = jnp.sum(jnp.where(placing == home_ids, jnp.arange(total_reqs, dtype=jnp.int32), 0))
    source_group = source // group_reqs
    from_group = jnp.arange(dp_size, dtype=jnp.int32)[None, :] == source_group
    proj_home = choose_rows(from_group, inbound)
    hidden_dec = (resid_dec.astype(F32) + proj_home.astype(F32)).astype(BF16)
    route_weight = route_scale / jnp.sum(route_scale, axis=-1, keepdims=True)
    expert_ids = jnp.arange(experts, dtype=jnp.int32)
    hits = routes[:, :, None] == expert_ids[None, None, :]
    weight_of = jnp.sum(jnp.where(hits, route_weight[:, :, None], 0.0), axis=1)
    moe_rows = jnp.concatenate([x_pre, hidden_dec], axis=0)
    rows_dev = moe_rows.shape[0]
    top_count = routes.shape[1]
    capacity = min(2 * rows_dev * top_count // experts, rows_dev)
    routed = jnp.any(hits, axis=1)
    row_ids = jnp.arange(rows_dev, dtype=jnp.int32)
    before = (row_ids[None, :] < row_ids[:, None]).astype(BF16)
    position = jnp.dot(before, routed.astype(BF16), preferred_element_type=F32).astype(jnp.int32)
    slot_ids_e = jnp.arange(capacity, dtype=jnp.int32)
    pick = routed[:, :, None] & (position[:, :, None] == slot_ids_e[None, None, :])
    pick_table = pick.reshape(rows_dev, experts * capacity)
    rows_f32 = moe_rows.astype(F32)
    normed = rms(rows_f32, moe_gain)
    outgoing = lax.dot_general(
        pick_table.astype(BF16), normed, (((0,), (0,)), ((), ())), preferred_element_type=F32
    ).astype(BF16)
    received = swap(outgoing.reshape(experts, capacity, width), "tp")
    expert_out = expert_units(received.reshape(experts * capacity, width), units)
    returned = swap(expert_out.reshape(experts, capacity, width), "tp")
    flat_back = returned.reshape(experts * capacity, width)
    high, middle, low = pieces_of(weight_of)

    def mix(piece):
        table = jnp.where(pick, piece[:, :, None], no_value)
        return jnp.dot(
            table.reshape(rows_dev, experts * capacity), flat_back, preferred_element_type=F32
        )

    moe_out = (rows_f32 + (mix(high) + mix(middle) + mix(low))).astype(BF16)
    return (moe_out[: rows_dev - 1], moe_out[rows_dev - 1 :])


def solution(mesh):
    placed = (
        P(("dp", "tp"), None),
        P(("dp", "tp"), None),
        P(("dp", "tp"), None),
        P(),
        P("dp"),
        P("dp"),
        P("dp", None, "tp", None),
        P("dp", None, "tp", None),
        P(None, "tp"),
        P(("dp", "tp"), None),
        P(("dp", "tp"), None),
        P(("dp", "tp"), None),
        P(),
        P("tp", "dp", None),
        P("tp", "dp", None),
        P("tp", "dp", None),
    )
    return jax.shard_map(
        on_device,
        mesh=mesh,
        in_specs=placed,
        out_specs=(P(("dp", "tp"), None), P(("dp", "tp"), None)),
        check_vma=False,
    )
```

profile of v0, /device:TPU:2, one launch (start us, length us, event | category | flops | bytes accessed | tf_op | source)
XLA Modules:
  0.0 313.3 jit_solution(5747145062844890888)
XLA Ops:
  7.2 0.0 all-gather.3.cloned.1.call-start
  7.3 0.7 all-gather.3.cloned.1.call-update
  8.0 0.0 all-gather.5.cloned.1.call-start
  8.0 2.0 pad_maximum_fusion
  10.0 93.1 %all-gather.3.cloned.1.call-done = bf16[1536,1536]{1,0:T(8,128)(2,1)} async-done(((bf16[48,1536]{1,0:T(8,128)(2,1)}), bf16[1536,1536]{1,0:T(8,128)(2,1)}) %all-gather.3.cloned.1.call-update) | async-done | bytes 4718608 | tf_op jit(solution)/shard_map/all_gather | solution.py:78
  103.1 0.0 all-gather.5.cloned.1.call-update
  103.1 0.7 maximum_reduce_fusion
  103.9 16.0 %all_to_all.40 = bf16[32,1,128]{2,1,0:T(2,128)(2,1)S(1)} all-to-all(bf16[32,1,128]{2,1,0:T(2,128)(2,1)S(1)} %copy.71), channel_id=1, replica_groups=mesh['dp'=16,'tp'=32] {'tp'}, dimensions={0} | all-to-all | bytes 16384 | tf_op jit(solution)/shard_map/all_to_all | solution.py:18
  119.9 0.7 broadcast_in_dim.175
  120.6 7.5 %all-to-all-start.1 = ((bf16[16,32,128]{2,1,0:T(8,128)(2,1)}), bf16[16,32,128]{2,1,0:T(8,128)(2,1)S(1)}, u32[]{:S(2)}, u32[]{:S(2)}) async-start(bf16[16,32,128]{2,1,0:T(8,128)(2,1)} %broadcast_in_dim.175), calls=%async_computation.1 | async-start | bytes 262144 | tf_op jit(solution)/shard_map/all_to_all | solution.py:18
  128.1 0.1 dynamic_slice.11
  128.2 0.1 fusion.65
  128.3 10.4 %all-to-all-done.1 = bf16[16,32,128]{2,1,0:T(8,128)(2,1)S(1)} async-done(((bf16[16,32,128]{2,1,0:T(8,128)(2,1)}), bf16[16,32,128]{2,1,0:T(8,128)(2,1)S(1)}, u32[]{:S(2)}, u32[]{:S(2)}) %all-to-all-start.1) | async-done | bytes 131104 | tf_op jit(solution)/shard_map/all_to_all | solution.py:18
  138.7 0.2 convolution_convert_fusion.5
  138.9 0.7 broadcast_in_dim.176
  139.6 5.1 %all-to-all-start.2 = ((bf16[32,16,128]{2,1,0:T(8,128)(2,1)}), bf16[32,16,128]{2,1,0:T(8,128)(2,1)S(1)}, u32[]{:S(2)}, u32[]{:S(2)}) async-start(bf16[32,16,128]{2,1,0:T(8,128)(2,1)} %broadcast_in_dim.176), calls=%async_computation.2 | async-start | bytes 262144 | tf_op jit(solution)/shard_map/all_to_all | solution.py:18
  144.7 0.6 dynamic_slice.10
  147.3 0.1 pad.17.clone
  147.4 0.0 copy-done.8
  147.4 0.1 broadcast_compare_fusion.1
  147.4 6.6 %all-to-all-done.2 = bf16[32,16,128]{2,1,0:T(8,128)(2,1)S(1)} async-done(((bf16[32,16,128]{2,1,0:T(8,128)(2,1)}), bf16[32,16,128]{2,1,0:T(8,128)(2,1)S(1)}, u32[]{:S(2)}, u32[]{:S(2)}) %all-to-all-start.2) | async-done | bytes 131104 | tf_op jit(solution)/shard_map/all_to_all | solution.py:18
  154.2 1.1 fusion.76
  155.3 0.1 copy.76
  155.4 1.3 convolution_convert_fusion.3
  156.7 0.1 copy.84
  156.8 0.3 fusion.22
  157.1 0.1 copy.78
  157.2 0.1 copy.85
  157.3 0.1 maximum_maximum_fusion
  157.4 0.7 copy.80
  158.1 5.7 %all-to-all-start.3 = ((bf16[32,16,128]{2,1,0:T(8,128)(2,1)}), bf16[32,16,128]{2,1,0:T(8,128)(2,1)S(1)}, u32[]{:S(2)}, u32[]{:S(2)}) async-start(bf16[32,16,128]{2,1,0:T(8,128)(2,1)} %copy.80), calls=%async_computation.3 | async-start | bytes 262144 | tf_op jit(solution)/shard_map/all_to_all | solution.py:18
  163.9 0.1 convolution_convert_fusion.4
  164.0 8.8 %all-to-all-done.3 = bf16[32,16,128]{2,1,0:T(8,128)(2,1)S(1)} async-done(((bf16[32,16,128]{2,1,0:T(8,128)(2,1)}), bf16[32,16,128]{2,1,0:T(8,128)(2,1)S(1)}, u32[]{:S(2)}, u32[]{:S(2)}) %all-to-all-start.3) | async-done | bytes 131104 | tf_op jit(solution)/shard_map/all_to_all | solution.py:18
  172.9 0.1 slice_add_fusion
  173.1 0.1 multiply_reduce_fusion
  173.2 0.1 fusion.61
  173.3 0.0 copy-start.5
  173.3 0.0 copy-start
  173.4 0.0 copy-start.2
  173.4 3.7 %convolution_reduce_fusion.1 = bf16[1536]{0:T(1024)(128)(2,1)S(1)} fusion(bf16[1536,1]{0,1:T(2,128)(2,1)S(1)} %reshape.225, bf16[1536,1536]{1,0:T(8,128)(2,1)} %all-gather.3.cloned.1.call-done), kind=kOutput, calls=%fused_computation.21 | convolution fusion | flops 4718592 | bytes 4724736 | tf_op jit(solution)/shard_map/dot_general | solution.py:12
  177.1 0.8 broadcast_select_fusion
  177.9 5.4 %all-to-all-start.4 = ((bf16[32,12,128]{2,1,0:T(8,128)(2,1)}), bf16[32,12,128]{2,1,0:T(8,128)(2,1)S(1)}, u32[]{:S(2)}, u32[]{:S(2)}) async-start(bf16[32,12,128]{2,1,0:T(8,128)(2,1)} %broadcast_select_fusion), calls=%async_computation.4 | async-start | bytes 262144 | tf_op jit(solution)/shard_map/all_to_all | solution.py:18
  183.3 0.1 and_select_fusion.1
  183.4 8.9 %all-to-all-done.4 = bf16[32,12,128]{2,1,0:T(8,128)(2,1)S(1)} async-done(((bf16[32,12,128]{2,1,0:T(8,128)(2,1)}), bf16[32,12,128]{2,1,0:T(8,128)(2,1)S(1)}, u32[]{:S(2)}, u32[]{:S(2)}) %all-to-all-start.4) | async-done | bytes 98336 | tf_op jit(solution)/shard_map/all_to_all | solution.py:18
  192.3 0.1 convolution_convert_fusion.2
  192.4 0.7 reshape.219
  193.1 3.5 %all-to-all-start.5 = ((bf16[16,12,128]{2,1,0:T(8,128)(2,1)}), bf16[16,12,128]{2,1,0:T(8,128)(2,1)S(1)}, u32[]{:S(2)}, u32[]{:S(2)}) async-start(bf16[16,12,128]{2,1,0:T(8,128)(2,1)} %reshape.219), calls=%async_computation.5 | async-start | bytes 131072 | tf_op jit(solution)/shard_map/all_to_all | solution.py:18
  196.6 0.6 select_reduce_fusion.1
  199.9 0.1 eq.153
  199.9 0.1 fusion.21
  200.1 4.3 %all-to-all-done.5 = bf16[16,12,128]{2,1,0:T(8,128)(2,1)S(1)} async-done(((bf16[16,12,128]{2,1,0:T(8,128)(2,1)}), bf16[16,12,128]{2,1,0:T(8,128)(2,1)S(1)}, u32[]{:S(2)}, u32[]{:S(2)}) %all-to-all-start.5) | async-done | bytes 49184 | tf_op jit(solution)/shard_map/all_to_all | solution.py:18
  204.4 0.1 convolution_reduce_fusion
  204.6 0.1 fusion.14
  204.7 0.6 convolution_convert_fusion.1
  205.4 44.8 %all_to_all.41 = bf16[32,16,1536]{2,1,0:T(8,128)(2,1)S(1)} all-to-all(bf16[32,16,1536]{2,1,0:T(8,128)(2,1)S(1)} %bitcast.91), channel_id=1, replica_groups=mesh['dp'=16,'tp'=32] {'tp'}, dimensions={0} | all-to-all | bytes 3145728 | tf_op jit(solution)/shard_map/all_to_all | solution.py:18
  250.2 3.1 fusion
  253.3 6.8 %convolution_convert_fusion = bf16[512,1536]{1,0:T(8,128)(2,1)} fusion(bf16[3,768,1536]{2,1,0:T(8,128)(2,1)} %all-gather.5.cloned.1.call-done, f32[512,768]{1,0:T(8,128)S(1)} %fusion, bf16[512,1536]{1,0:T(8,128)(2,1)S(1)} %bitcast.93), kind=kOutput, calls=%fused_computation | convolution fusion | flops 2417885184 | bytes 9437184 | tf_op jit(solution)/shard_map/dot_general | solution.py:46
  260.0 5.7 %all-to-all-start.7 = ((bf16[32,16,1536]{2,1,0:T(8,128)(2,1)}), bf16[32,16,1536]{2,1,0:T(8,128)(2,1)S(1)}, u32[]{:S(2)}, u32[]{:S(2)}) async-start(bf16[32,16,1536]{2,1,0:T(8,128)(2,1)} %bitcast.24), calls=%async_computation.7 | async-start | bytes 3145728 | tf_op jit(solution)/shard_map/all_to_all | solution.py:18
  265.8 38.6 %all-to-all-done.7 = bf16[32,16,1536]{2,1,0:T(8,128)(2,1)S(1)} async-done(((bf16[32,16,1536]{2,1,0:T(8,128)(2,1)}), bf16[32,16,1536]{2,1,0:T(8,128)(2,1)S(1)}, u32[]{:S(2)}, u32[]{:S(2)}) %all-to-all-start.7) | async-done | bytes 1572896 | tf_op jit(solution)/shard_map/all_to_all | solution.py:18
  304.4 0.4 convolution_bitcast_fusion.2
  304.9 0.4 fusion.4
  305.3 0.4 fusion.5
  305.7 0.0 copy-start.1
  305.7 0.7 slice.74
  (49 shorter events, 0.5 us)
Async XLA Ops:
  7.2 121.0 %copy-start.6 = (s32[512]{0:T(512)S(1)}, s32[512]{0:T(512)}, u32[]{:S(2)}) copy-start(s32[512]{0:T(512)} %param.19) | copy-start | bytes 6148
  7.2 121.1 %copy-start.3 = (s32[64,4]{0,1:T(4,128)S(1)}, s32[64,4]{0,1:T(4,128)}, u32[]{:S(2)}) copy-start(s32[64,4]{0,1:T(4,128)} %param.26) | copy-start | bytes 3076
  7.2 140.2 %copy-start.7 = (s32[32]{0:T(128)S(1)}, s32[32]{0:T(128)}, u32[]{:S(2)}) copy-start(s32[32]{0:T(128)} %param.20) | copy-start | bytes 388
  7.2 140.2 %copy-start.8 = (s32[32]{0:T(128)S(1)}, s32[32]{0:T(128)}, u32[]{:S(2)}) copy-start(s32[32]{0:T(128)} %param.21) | copy-start | bytes 388
  7.2 95.9 %all-gather.3.cloned.1.call-start = ((), (), s32[]{:S(2)}) async-start(), calls=%async_computation.8 | async-start | bytes 4866048 | tf_op jit(solution)/shard_map/all_gather | solution.py:78
  7.9 146.2 %copy-start.9 = (bf16[32,2,64,128]{3,2,1,0:T(8,128)(2,1)S(1)}, bf16[32,2,64,128]{3,2,1,0:T(8,128)(2,1)}, u32[]{:S(2)}) copy-start(bf16[32,2,64,128]{3,2,1,0:T(8,128)(2,1)} %param.22) | copy-start | bytes 3145732
  8.0 242.2 %all-gather.5.cloned.1.call-start = ((), (), s32[]{:S(2)}) async-start(), calls=%async_computation.9 | async-start | bytes 7520256 | tf_op jit(solution)/shard_map/all_gather | solution.py:81
  120.6 18.1 %all-to-all-start.1 = ((bf16[16,32,128]{2,1,0:T(8,128)(2,1)}), bf16[16,32,128]{2,1,0:T(8,128)(2,1)S(1)}, u32[]{:S(2)}, u32[]{:S(2)}) async-start(bf16[16,32,128]{2,1,0:T(8,128)(2,1)} %broadcast_in_dim.175), calls=%async_computation.1 | async-start | bytes 262144 | tf_op jit(solution)/shard_map/all_to_all | solution.py:18
  138.9 16.5 %copy-start.10 = (bf16[32,2,64,128]{3,2,1,0:T(8,128)(2,1)S(1)}, bf16[32,2,64,128]{3,2,1,0:T(8,128)(2,1)}, u32[]{:S(2)}) copy-start(bf16[32,2,64,128]{3,2,1,0:T(8,128)(2,1)} %param.23) | copy-start | bytes 3145732
  139.6 14.5 %all-to-all-start.2 = ((bf16[32,16,128]{2,1,0:T(8,128)(2,1)}), bf16[32,16,128]{2,1,0:T(8,128)(2,1)S(1)}, u32[]{:S(2)}, u32[]{:S(2)}) async-start(bf16[32,16,128]{2,1,0:T(8,128)(2,1)} %broadcast_in_dim.176), calls=%async_computation.2 | async-start | bytes 262144 | tf_op jit(solution)/shard_map/all_to_all | solution.py:18
  158.1 14.7 %all-to-all-start.3 = ((bf16[32,16,128]{2,1,0:T(8,128)(2,1)}), bf16[32,16,128]{2,1,0:T(8,128)(2,1)S(1)}, u32[]{:S(2)}, u32[]{:S(2)}) async-start(bf16[32,16,128]{2,1,0:T(8,128)(2,1)} %copy.80), calls=%async_computation.3 | async-start | bytes 262144 | tf_op jit(solution)/shard_map/all_to_all | solution.py:18
  173.3 31.2 %copy-start.5 = (bf16[1,1536]{1,0:T(2,128)(2,1)S(1)}, bf16[1,1536]{1,0:T(2,128)(2,1)}, u32[]{:S(2)}) copy-start(bf16[1,1536]{1,0:T(2,128)(2,1)} %param.18) | copy-start | bytes 9220
  173.3 31.2 %copy-start = (bf16[63,1536]{1,0:T(8,128)(2,1)S(1)}, bf16[63,1536]{1,0:T(8,128)(2,1)}, u32[]{:S(2)}) copy-start(bf16[63,1536]{1,0:T(8,128)(2,1)} %param.25) | copy-start | bytes 580612
  173.4 31.4 %copy-start.2 = (f32[1536]{0:T(1024)S(1)}, f32[1536]{0:T(1024)}, u32[]{:S(2)}) copy-start(f32[1536]{0:T(1024)} %param.28) | copy-start | bytes 18436
  177.9 14.4 %all-to-all-start.4 = ((bf16[32,12,128]{2,1,0:T(8,128)(2,1)}), bf16[32,12,128]{2,1,0:T(8,128)(2,1)S(1)}, u32[]{:S(2)}, u32[]{:S(2)}) async-start(bf16[32,12,128]{2,1,0:T(8,128)(2,1)} %broadcast_select_fusion), calls=%async_computation.4 | async-start | bytes 262144 | tf_op jit(solution)/shard_map/all_to_all | solution.py:18
  193.1 11.3 %all-to-all-start.5 = ((bf16[16,12,128]{2,1,0:T(8,128)(2,1)}), bf16[16,12,128]{2,1,0:T(8,128)(2,1)S(1)}, u32[]{:S(2)}, u32[]{:S(2)}) async-start(bf16[16,12,128]{2,1,0:T(8,128)(2,1)} %reshape.219), calls=%async_computation.5 | async-start | bytes 131072 | tf_op jit(solution)/shard_map/all_to_all | solution.py:18
  260.0 5.7 %copy-start.4 = (f32[64,4]{0,1:T(4,128)S(1)}, f32[64,4]{0,1:T(4,128)}, u32[]{:S(2)}) copy-start(f32[64,4]{0,1:T(4,128)} %param.27) | copy-start | bytes 3076
  260.0 44.4 %all-to-all-start.7 = ((bf16[32,16,1536]{2,1,0:T(8,128)(2,1)}), bf16[32,16,1536]{2,1,0:T(8,128)(2,1)S(1)}, u32[]{:S(2)}, u32[]{:S(2)}) async-start(bf16[32,16,1536]{2,1,0:T(8,128)(2,1)} %bitcast.24), calls=%async_computation.7 | async-start | bytes 3145728 | tf_op jit(solution)/shard_map/all_to_all | solution.py:18
  305.7 0.7 copy-start.1
Sparse Core Ops, SparseCore 0:
  11.2 91.8 all-gather.2
  105.2 55.1 all-gather.4
where the time goes:
time: 314 us; the launch traced here: 313 us
  waiting for transfers between devices  171 us (54%)
  blocking collectives  60.8 us (19%)
  starting transfers between devices  33 us (11%)
  between operations  19 us (6%)
  matrix products  18.5 us (6%)
  other arithmetic  5.56 us (2%)
  local copies, waits for them, and re-layouts  4.87 us (2%)
    all_gather x1, waiting for transfers between devices, on_device(): out_rows = lax.all_gather(w_out.T, 'tp', axis=0, tiled=True)  93.1 us
    all_to_all x6, waiting for transfers between devices, swap(): lax.all_to_all(blocks, axis_name, split_axis=0, concat_axis=0, tiled=True)  77.6 us
    all_to_all x2, blocking collectives, swap(): lax.all_to_all(blocks, axis_name, split_axis=0, concat_axis=0, tiled=True)  60.8 us
    all_to_all x6, starting transfers between devices, swap(): lax.all_to_all(blocks, axis_name, split_axis=0, concat_axis=0, tiled=True)  33 us
    dot_general x2, matrix products, contract_rows(): lax.dot_general(left_rows, unit_rows, (((1,), (1,)), ((), ())), preferred...  6.79 us
    dot_general x1, matrix products, expert_units(): return jnp.dot(active, units[2], preferred_element_type=F32).astype(BF16)  6.77 us
  transfers between devices with their start and end apart: 8, of which 7 were waited for; matrix products, arithmetic and copies ran while one was open for 5% of the time, Pallas kernels for 0%

commit v1 on v0

--- a/solution.py
+++ b/solution.py
@@ -75,7 +75,9 @@
     total_reqs = placing.shape[0]
     experts = tp_size * w_gate.shape[0]
     assert group_reqs == tp_size and experts == tp_size
-    out_rows = lax.all_gather(w_out.T, "tp", axis=0, tiled=True)
+    out_rows = jnp.concatenate(
+        lax.all_to_all(jnp.stack([w_out.T] * lax.axis_size("tp")), "tp", 0, 0), axis=0
+    )
     stacked = jnp.concatenate([w_gate, w_up, w_down], axis=0)
     stacked, _ = lax.optimization_barrier((stacked, out_rows))
     units = lax.all_gather(stacked, "dp", axis=1, tiled=True)

time: 314 us -> 341 us (1.086)
  starting transfers between devices: 33 us -> 47.7 us
  waiting for transfers between devices: 171 us -> 185 us
  local copies, waits for them, and re-layouts: 4.87 us -> 8.45 us
    all_to_all x0 -> x1, waiting for transfers between devices: none -> 107 us  [on_device(): lax.all_to_all(jnp.stack([w_out.T] * lax.axis_size('tp')), 'tp', 0, 0)]
    all_gather x1 -> x0, waiting for transfers between devices: 93.1 us -> none  [on_device(): out_rows = lax.all_gather(w_out.T, 'tp', axis=0, tiled=True)]
    all_to_all x0 -> x1, starting transfers between devices: none -> 10.5 us  [on_device(): lax.all_to_all(jnp.stack([w_out.T] * lax.axis_size('tp')), 'tp', 0, 0)]
    all_to_all x6, starting transfers between devices: 33 us -> 37.1 us  [swap(): lax.all_to_all(blocks, axis_name, split_axis=0, concat_axis=0, tiled=True)]
    another operation x0 -> x1, local copies, waits for them, and re-layouts: none -> 3.56 us  [on_device(): jnp.stack([w_out.T] * lax.axis_size('tp'))]
  transfers between devices with their start and end apart: 8 -> 8, of which waited for: 7 -> 7; matrix products, arithmetic and copies ran while one was open for 5% -> 4% of each run, Pallas kernels for 0% -> 0%
where the time goes in v1:
time: 341 us; the launch traced here: 340 us
  waiting for transfers between devices  185 us (54%)
  blocking collectives  57.8 us (17%)
  starting transfers between devices  47.7 us (14%)
  between operations  19.1 us (6%)
  matrix products  18.5 us (5%)
  local copies, waits for them, and re-layouts  8.45 us (2%)
  other arithmetic  3.72 us (1%)
    all_to_all x1, waiting for transfers between devices, on_device(): lax.all_to_all(jnp.stack([w_out.T] * lax.axis_size('tp')), 'tp', 0, 0)  107 us
    all_to_all x6, waiting for transfers between devices, swap(): lax.all_to_all(blocks, axis_name, split_axis=0, concat_axis=0, tiled=True)  77.5 us
    all_to_all x2, blocking collectives, swap(): lax.all_to_all(blocks, axis_name, split_axis=0, concat_axis=0, tiled=True)  57.8 us
    all_to_all x6, starting transfers between devices, swap(): lax.all_to_all(blocks, axis_name, split_axis=0, concat_axis=0, tiled=True)  37.1 us
    all_to_all x1, starting transfers between devices, on_device(): lax.all_to_all(jnp.stack([w_out.T] * lax.axis_size('tp')), 'tp', 0, 0)  10.5 us
  transfers between devices with their start and end apart: 8, of which 7 were waited for; matrix products, arithmetic and copies ran while one was open for 4% of the time, Pallas kernels for 0%

profile of v1, /device:TPU:2, one launch (start us, length us, event | category | flops | bytes accessed | tf_op | source)
XLA Modules:
  0.0 339.8 jit_solution(2811960859565092823)
XLA Ops:
  7.2 3.6 %stack.2 = bf16[32,48,1536]{2,1,0:T(8,128)(2,1)} broadcast(bf16[48,1536]{1,0:T(8,128)(2,1)} %bitcast.101), dimensions={1,2} | broadcast | bytes 4866048 | tf_op jit(solution)/shard_map/stack | solution.py:79
  10.7 0.0 copy-start.11
  10.7 10.5 %all-to-all-start.4 = ((bf16[32,48,1536]{2,1,0:T(8,128)(2,1)}), bf16[32,48,1536]{2,1,0:T(8,128)(2,1)}, u32[]{:S(2)}, u32[]{:S(2)}) async-start(bf16[32,48,1536]{2,1,0:T(8,128)(2,1)} %stack.2), calls=%async_computation.4 | async-start | bytes 9437184 | tf_op jit(solution)/shard_map/all_to_all | solution.py:79
  21.3 0.0 copy-start.10
  21.3 0.0 copy-start.6
  21.3 0.0 copy-start.14
  21.3 0.0 all-gather.2.cloned.1.call-start
  21.4 0.8 pad_maximum_fusion
  22.2 107.1 %all-to-all-done.4 = bf16[32,48,1536]{2,1,0:T(8,128)(2,1)} async-done(((bf16[32,48,1536]{2,1,0:T(8,128)(2,1)}), bf16[32,48,1536]{2,1,0:T(8,128)(2,1)}, u32[]{:S(2)}, u32[]{:S(2)}) %all-to-all-start.4) | async-done | bytes 4718624 | tf_op jit(solution)/shard_map/all_to_all | solution.py:79
  129.3 0.0 all-gather.2.cloned.1.call-update
  129.5 13.0 %all_to_all.45 = bf16[32,1,128]{2,1,0:T(2,128)(2,1)S(1)} all-to-all(bf16[32,1,128]{2,1,0:T(2,128)(2,1)S(1)} %copy.71), channel_id=1, replica_groups=mesh['dp'=16,'tp'=32] {'tp'}, dimensions={0} | all-to-all | bytes 16384 | tf_op jit(solution)/shard_map/all_to_all | solution.py:18
  142.4 0.7 broadcast_in_dim.175
  143.1 11.7 %all-to-all-start.1 = ((bf16[16,32,128]{2,1,0:T(8,128)(2,1)}), bf16[16,32,128]{2,1,0:T(8,128)(2,1)S(1)}, u32[]{:S(2)}, u32[]{:S(2)}) async-start(bf16[16,32,128]{2,1,0:T(8,128)(2,1)} %broadcast_in_dim.175), calls=%async_computation.1 | async-start | bytes 262144 | tf_op jit(solution)/shard_map/all_to_all | solution.py:18
  154.9 0.1 dynamic_slice.11
  155.0 0.1 fusion.65
  155.1 10.5 %all-to-all-done.1 = bf16[16,32,128]{2,1,0:T(8,128)(2,1)S(1)} async-done(((bf16[16,32,128]{2,1,0:T(8,128)(2,1)}), bf16[16,32,128]{2,1,0:T(8,128)(2,1)S(1)}, u32[]{:S(2)}, u32[]{:S(2)}) %all-to-all-start.1) | async-done | bytes 131104 | tf_op jit(solution)/shard_map/all_to_all | solution.py:18
  165.5 0.2 convolution_convert_fusion.5
  165.7 0.7 broadcast_in_dim.176
  166.4 5.0 %all-to-all-start.2 = ((bf16[32,16,128]{2,1,0:T(8,128)(2,1)}), bf16[32,16,128]{2,1,0:T(8,128)(2,1)S(1)}, u32[]{:S(2)}, u32[]{:S(2)}) async-start(bf16[32,16,128]{2,1,0:T(8,128)(2,1)} %broadcast_in_dim.176), calls=%async_computation.2 | async-start | bytes 262144 | tf_op jit(solution)/shard_map/all_to_all | solution.py:18
  171.5 0.6 dynamic_slice.10
  174.0 0.1 pad.17.clone
  174.1 0.1 broadcast_compare_fusion.1
  174.2 6.6 %all-to-all-done.2 = bf16[32,16,128]{2,1,0:T(8,128)(2,1)S(1)} async-done(((bf16[32,16,128]{2,1,0:T(8,128)(2,1)}), bf16[32,16,128]{2,1,0:T(8,128)(2,1)S(1)}, u32[]{:S(2)}, u32[]{:S(2)}) %all-to-all-start.2) | async-done | bytes 131104 | tf_op jit(solution)/shard_map/all_to_all | solution.py:18
  180.9 1.1 fusion.76
  182.1 0.1 copy.76
  182.1 0.3 fusion.22
  182.4 0.1 copy.78
  182.6 0.1 copy.85
  182.7 0.1 copy.84
  182.8 1.3 convolution_convert_fusion.3
  184.1 0.1 maximum_maximum_fusion
  184.2 0.7 copy.80
  184.9 5.7 %all-to-all-start.3 = ((bf16[32,16,128]{2,1,0:T(8,128)(2,1)}), bf16[32,16,128]{2,1,0:T(8,128)(2,1)S(1)}, u32[]{:S(2)}, u32[]{:S(2)}) async-start(bf16[32,16,128]{2,1,0:T(8,128)(2,1)} %copy.80), calls=%async_computation.3 | async-start | bytes 262144 | tf_op jit(solution)/shard_map/all_to_all | solution.py:18
  190.6 0.1 convolution_convert_fusion.4
  190.8 8.8 %all-to-all-done.3 = bf16[32,16,128]{2,1,0:T(8,128)(2,1)S(1)} async-done(((bf16[32,16,128]{2,1,0:T(8,128)(2,1)}), bf16[32,16,128]{2,1,0:T(8,128)(2,1)S(1)}, u32[]{:S(2)}, u32[]{:S(2)}) %all-to-all-start.3) | async-done | bytes 131104 | tf_op jit(solution)/shard_map/all_to_all | solution.py:18
  199.6 0.1 slice_add_fusion
  199.9 0.1 multiply_reduce_fusion
  200.0 0.1 fusion.61
  200.1 0.0 copy-start
  200.1 3.7 %convolution_reduce_fusion.1 = bf16[1536]{0:T(1024)(128)(2,1)S(1)} fusion(bf16[1536,1]{0,1:T(2,128)(2,1)S(1)} %reshape.241, bf16[1536,1536]{1,0:T(8,128)(2,1)} %bitcast.16), kind=kOutput, calls=%fused_computation.21 | convolution fusion | flops 4718592 | bytes 4724736 | tf_op jit(solution)/shard_map/dot_general | solution.py:12
  203.8 0.8 broadcast_select_fusion
  204.6 5.4 %all-to-all-start.5 = ((bf16[32,12,128]{2,1,0:T(8,128)(2,1)}), bf16[32,12,128]{2,1,0:T(8,128)(2,1)S(1)}, u32[]{:S(2)}, u32[]{:S(2)}) async-start(bf16[32,12,128]{2,1,0:T(8,128)(2,1)} %broadcast_select_fusion), calls=%async_computation.5 | async-start | bytes 262144 | tf_op jit(solution)/shard_map/all_to_all | solution.py:18
  210.0 0.1 and_select_fusion.1
  210.1 8.8 %all-to-all-done.5 = bf16[32,12,128]{2,1,0:T(8,128)(2,1)S(1)} async-done(((bf16[32,12,128]{2,1,0:T(8,128)(2,1)}), bf16[32,12,128]{2,1,0:T(8,128)(2,1)S(1)}, u32[]{:S(2)}, u32[]{:S(2)}) %all-to-all-start.5) | async-done | bytes 98336 | tf_op jit(solution)/shard_map/all_to_all | solution.py:18
  219.0 0.1 convolution_convert_fusion.2
  219.1 0.7 reshape.235
  219.8 3.5 %all-to-all-start.6 = ((bf16[16,12,128]{2,1,0:T(8,128)(2,1)}), bf16[16,12,128]{2,1,0:T(8,128)(2,1)S(1)}, u32[]{:S(2)}, u32[]{:S(2)}) async-start(bf16[16,12,128]{2,1,0:T(8,128)(2,1)} %reshape.235), calls=%async_computation.6 | async-start | bytes 131072 | tf_op jit(solution)/shard_map/all_to_all | solution.py:18
  223.3 0.6 select_reduce_fusion.1
  226.5 0.1 eq.153
  226.6 0.1 fusion.21
  226.8 4.3 %all-to-all-done.6 = bf16[16,12,128]{2,1,0:T(8,128)(2,1)S(1)} async-done(((bf16[16,12,128]{2,1,0:T(8,128)(2,1)}), bf16[16,12,128]{2,1,0:T(8,128)(2,1)S(1)}, u32[]{:S(2)}, u32[]{:S(2)}) %all-to-all-start.6) | async-done | bytes 49184 | tf_op jit(solution)/shard_map/all_to_all | solution.py:18
  231.1 0.1 convolution_reduce_fusion
  231.2 0.1 fusion.14
  231.4 0.6 convolution_convert_fusion.1
  232.1 44.8 %all_to_all.46 = bf16[32,16,1536]{2,1,0:T(8,128)(2,1)S(1)} all-to-all(bf16[32,16,1536]{2,1,0:T(8,128)(2,1)S(1)} %bitcast.92), channel_id=1, replica_groups=mesh['dp'=16,'tp'=32] {'tp'}, dimensions={0} | all-to-all | bytes 3145728 | tf_op jit(solution)/shard_map/all_to_all | solution.py:18
  276.9 3.1 fusion
  280.0 6.8 %convolution_convert_fusion = bf16[512,1536]{1,0:T(8,128)(2,1)} fusion(bf16[3,768,1536]{2,1,0:T(8,128)(2,1)} %all-gather.2.cloned.1.call-done, f32[512,768]{1,0:T(8,128)S(1)} %fusion, bf16[512,1536]{1,0:T(8,128)(2,1)S(1)} %bitcast.94), kind=kOutput, calls=%fused_computation | convolution fusion | flops 2417885184 | bytes 9437184 | tf_op jit(solution)/shard_map/dot_general | solution.py:46
  286.7 5.7 %all-to-all-start.8 = ((bf16[32,16,1536]{2,1,0:T(8,128)(2,1)}), bf16[32,16,1536]{2,1,0:T(8,128)(2,1)S(1)}, u32[]{:S(2)}, u32[]{:S(2)}) async-start(bf16[32,16,1536]{2,1,0:T(8,128)(2,1)} %bitcast.25), calls=%async_computation.8 | async-start | bytes 3145728 | tf_op jit(solution)/shard_map/all_to_all | solution.py:18
  292.5 38.4 %all-to-all-done.8 = bf16[32,16,1536]{2,1,0:T(8,128)(2,1)S(1)} async-done(((bf16[32,16,1536]{2,1,0:T(8,128)(2,1)}), bf16[32,16,1536]{2,1,0:T(8,128)(2,1)S(1)}, u32[]{:S(2)}, u32[]{:S(2)}) %all-to-all-start.8) | async-done | bytes 1572896 | tf_op jit(solution)/shard_map/all_to_all | solution.py:18
  331.0 0.4 convolution_bitcast_fusion.2
  331.4 0.4 fusion.4
  331.8 0.4 fusion.5
  332.3 0.7 slice.74
  333.0 0.0 copy-done.1
  (59 shorter events, 0.5 us)
Async XLA Ops:
  10.7 10.6 %copy-start.2 = (bf16[1,48,1536]{2,1,0:T(8,128)(2,1)S(1)}, bf16[1,48,1536]{2,1,0:T(8,128)(2,1)}, u32[]{:S(2)}) copy-start(bf16[1,48,1536]{2,1,0:T(8,128)(2,1)} %param.31) | copy-start | bytes 442372
  10.7 10.7 %copy-start.3 = (bf16[1,48,1536]{2,1,0:T(8,128)(2,1)S(1)}, bf16[1,48,1536]{2,1,0:T(8,128)(2,1)}, u32[]{:S(2)}) copy-start(bf16[1,48,1536]{2,1,0:T(8,128)(2,1)} %param.30) | copy-start | bytes 442372
  10.7 10.7 %copy-start.4 = (bf16[1,48,1536]{2,1,0:T(8,128)(2,1)S(1)}, bf16[1,48,1536]{2,1,0:T(8,128)(2,1)}, u32[]{:S(2)}) copy-start(bf16[1,48,1536]{2,1,0:T(8,128)(2,1)} %param.29) | copy-start | bytes 442372
  10.7 118.6 %copy-start.8 = (bf16[1,1536]{1,0:T(2,128)(2,1)S(1)}, bf16[1,1536]{1,0:T(2,128)(2,1)}, u32[]{:S(2)}) copy-start(bf16[1,1536]{1,0:T(2,128)(2,1)} %param.16) | copy-start | bytes 9220
  10.7 118.6 %copy-start.11 = (bf16[1,512]{1,0:T(2,128)(2,1)S(1)}, bf16[1,512]{1,0:T(2,128)(2,1)}, u32[]{:S(2)}) copy-start(bf16[1,512]{1,0:T(2,128)(2,1)} %param.17) | copy-start | bytes 3076
  10.7 118.6 %all-to-all-start.4 = ((bf16[32,48,1536]{2,1,0:T(8,128)(2,1)}), bf16[32,48,1536]{2,1,0:T(8,128)(2,1)}, u32[]{:S(2)}, u32[]{:S(2)}) async-start(bf16[32,48,1536]{2,1,0:T(8,128)(2,1)} %stack.2), calls=%async_computation.4 | async-start | bytes 9437184 | tf_op jit(solution)/shard_map/all_to_all | solution.py:79
  21.3 133.6 %copy-start.10 = (s32[512]{0:T(512)S(1)}, s32[512]{0:T(512)}, u32[]{:S(2)}) copy-start(s32[512]{0:T(512)} %param.19) | copy-start | bytes 6148
  21.3 133.8 %copy-start.6 = (s32[64,4]{0,1:T(4,128)S(1)}, s32[64,4]{0,1:T(4,128)}, u32[]{:S(2)}) copy-start(s32[64,4]{0,1:T(4,128)} %param.26) | copy-start | bytes 3076
  21.3 152.8 %copy-start.12 = (s32[32]{0:T(128)S(1)}, s32[32]{0:T(128)}, u32[]{:S(2)}) copy-start(s32[32]{0:T(128)} %param.20) | copy-start | bytes 388
  21.3 152.8 %copy-start.13 = (s32[32]{0:T(128)S(1)}, s32[32]{0:T(128)}, u32[]{:S(2)}) copy-start(s32[32]{0:T(128)} %param.21) | copy-start | bytes 388
  21.3 159.6 %copy-start.14 = (bf16[32,2,64,128]{3,2,1,0:T(8,128)(2,1)S(1)}, bf16[32,2,64,128]{3,2,1,0:T(8,128)(2,1)}, u32[]{:S(2)}) copy-start(bf16[32,2,64,128]{3,2,1,0:T(8,128)(2,1)} %param.22) | copy-start | bytes 3145732
  21.3 255.6 %all-gather.2.cloned.1.call-start = ((), (), s32[]{:S(2)}) async-start(), calls=%async_computation.9 | async-start | bytes 7520256 | tf_op jit(solution)/shard_map/all_gather | solution.py:83
  143.1 22.4 %all-to-all-start.1 = ((bf16[16,32,128]{2,1,0:T(8,128)(2,1)}), bf16[16,32,128]{2,1,0:T(8,128)(2,1)S(1)}, u32[]{:S(2)}, u32[]{:S(2)}) async-start(bf16[16,32,128]{2,1,0:T(8,128)(2,1)} %broadcast_in_dim.175), calls=%async_computation.1 | async-start | bytes 262144 | tf_op jit(solution)/shard_map/all_to_all | solution.py:18
  166.4 14.4 %all-to-all-start.2 = ((bf16[32,16,128]{2,1,0:T(8,128)(2,1)}), bf16[32,16,128]{2,1,0:T(8,128)(2,1)S(1)}, u32[]{:S(2)}, u32[]{:S(2)}) async-start(bf16[32,16,128]{2,1,0:T(8,128)(2,1)} %broadcast_in_dim.176), calls=%async_computation.2 | async-start | bytes 262144 | tf_op jit(solution)/shard_map/all_to_all | solution.py:18
  180.8 2.0 copy-start.15
  184.9 14.7 %all-to-all-start.3 = ((bf16[32,16,128]{2,1,0:T(8,128)(2,1)}), bf16[32,16,128]{2,1,0:T(8,128)(2,1)S(1)}, u32[]{:S(2)}, u32[]{:S(2)}) async-start(bf16[32,16,128]{2,1,0:T(8,128)(2,1)} %copy.80), calls=%async_computation.3 | async-start | bytes 262144 | tf_op jit(solution)/shard_map/all_to_all | solution.py:18
  200.1 31.1 %copy-start.9 = (bf16[1,1536]{1,0:T(2,128)(2,1)S(1)}, bf16[1,1536]{1,0:T(2,128)(2,1)}, u32[]{:S(2)}) copy-start(bf16[1,1536]{1,0:T(2,128)(2,1)} %param.18) | copy-start | bytes 9220
  200.1 31.1 %copy-start = (bf16[63,1536]{1,0:T(8,128)(2,1)S(1)}, bf16[63,1536]{1,0:T(8,128)(2,1)}, u32[]{:S(2)}) copy-start(bf16[63,1536]{1,0:T(8,128)(2,1)} %param.25) | copy-start | bytes 580612
  200.1 31.3 %copy-start.5 = (f32[1536]{0:T(1024)S(1)}, f32[1536]{0:T(1024)}, u32[]{:S(2)}) copy-start(f32[1536]{0:T(1024)} %param.28) | copy-start | bytes 18436
  204.6 14.3 %all-to-all-start.5 = ((bf16[32,12,128]{2,1,0:T(8,128)(2,1)}), bf16[32,12,128]{2,1,0:T(8,128)(2,1)S(1)}, u32[]{:S(2)}, u32[]{:S(2)}) async-start(bf16[32,12,128]{2,1,0:T(8,128)(2,1)} %broadcast_select_fusion), calls=%async_computation.5 | async-start | bytes 262144 | tf_op jit(solution)/shard_map/all_to_all | solution.py:18
  219.8 11.3 %all-to-all-start.6 = ((bf16[16,12,128]{2,1,0:T(8,128)(2,1)}), bf16[16,12,128]{2,1,0:T(8,128)(2,1)S(1)}, u32[]{:S(2)}, u32[]{:S(2)}) async-start(bf16[16,12,128]{2,1,0:T(8,128)(2,1)} %reshape.235), calls=%async_computation.6 | async-start | bytes 131072 | tf_op jit(solution)/shard_map/all_to_all | solution.py:18
  286.7 5.7 %copy-start.7 = (f32[64,4]{0,1:T(4,128)S(1)}, f32[64,4]{0,1:T(4,128)}, u32[]{:S(2)}) copy-start(f32[64,4]{0,1:T(4,128)} %param.27) | copy-start | bytes 3076
  286.7 44.2 %all-to-all-start.8 = ((bf16[32,16,1536]{2,1,0:T(8,128)(2,1)}), bf16[32,16,1536]{2,1,0:T(8,128)(2,1)S(1)}, u32[]{:S(2)}, u32[]{:S(2)}) async-start(bf16[32,16,1536]{2,1,0:T(8,128)(2,1)} %bitcast.25), calls=%async_computation.8 | async-start | bytes 3145728 | tf_op jit(solution)/shard_map/all_to_all | solution.py:18
  332.3 0.7 copy-start.1
Sparse Core Ops, SparseCore 0:
  129.5 56.3 all-gather.1
